TPU v7x, 32 devices: a whole 2x2x4 slice. The times are simulated.
32 devices in a mesh: depth: 4 (over z), lat: 8 (over y, x, core).
Axes of the slice: x: 2, y: 2, z: 4, core: 2. Of those that a mesh axis runs over, the one named last changes fastest.
Arguments:
- volume_init: float32 [16, 64, 16, 128], P('depth', 'lat'), may hold values from 0.2 to 10
- measured: float32 [64, 16, 128], P('lat'), may hold values from 0.25 to 4
- psf: bfloat16 [16, 13, 128, 128], P('depth'), may hold values from 0 to 0.0043269231
- offsets: int32 [16, 13], replicated, may hold values from 0 to 24, as said below
- counts: int32 [16], replicated, may hold values from 1 to 13, 130 in all
Outputs:
- volume: float32 [16, 64, 16, 128], P('depth', 'lat')
Inputs may be any that keep to these rules, and one draw needn't show every extreme that they name: `offsets`: entry v names the block offset (v // 5 - 2, v % 5 - 2) in patch rows and patches; the entries of one depth are distinct, and entry 0 of every depth is the central offset 2 * 5 + 2.
All inputs are finite; a program needn't handle non-finite values.
Results may differ from a plain program's by a relative error of at most 0.00076.
Values may be sent and summed in bfloat16 or wider, within the bound.
A program may use at most 64 MiB of HBM per device.

v0:
```python
import jax
import jax.numpy as jnp
from jax import lax
from jax.sharding import PartitionSpec as P

RY = 2
RX = 2
ITERS = 2


def with_halo(cells, sides, width):
    for axis, dim in sides:
        count = lax.axis_size(axis)
        ends = count - 1
        head = lax.slice_in_dim(cells, 0, width, axis=dim)
        tail = lax.slice_in_dim(cells, cells.shape[dim] - width, cells.shape[dim], axis=dim)
        cells = jnp.concatenate(
            [
                lax.ppermute(tail, axis, [(i, (i + 1) % count) for i in range(ends)]),
                cells,
                lax.ppermute(head, axis, [((i + 1) % count, i) for i in range(ends)]),
            ],
            axis=dim,
        )
    return cells


def split_offsets(offsets):
    span_x = 2 * RX + 1
    return (offsets // span_x - RY, offsets % span_x - RX)


def project(plane, blocks, rows_by, cols_by, transpose):
    plane_rows = plane.shape[0]
    plane_cols = plane.shape[1]
    tile_rows = plane_rows - 2 * RY
    tile_cols = plane_cols - 2 * RX
    pixels = plane.shape[2]
    flat_plane = plane.reshape(plane_rows * plane_cols, pixels)
    span_x = 2 * RX + 1
    span_all = (2 * RY + 1) * span_x
    codes = (rows_by + RY) * span_x + (cols_by + RX)
    one_hot = (codes[:, None] == jnp.arange(span_all, dtype=jnp.int32)[None, :]).astype(jnp.float32)
    block_values = blocks.astype(jnp.float32)
    if transpose:
        dense = jnp.einsum("ko,kji->ioj", one_hot, block_values, precision=lax.Precision.HIGHEST)
    else:
        dense = jnp.einsum("ko,kji->joi", one_hot, block_values, precision=lax.Precision.HIGHEST)
    dense = dense.astype(jnp.bfloat16).reshape(pixels, span_all * pixels)
    products = jnp.dot(flat_plane, dense, preferred_element_type=jnp.float32).reshape(
        plane_rows, plane_cols, span_all, pixels
    )
    total = jnp.zeros((tile_rows, tile_cols, pixels), jnp.float32)
    for code in range(span_all):
        row_start = code // span_x
        col_start = code % span_x
        total = (
            total
            + products[row_start : row_start + tile_rows, col_start : col_start + tile_cols, code]
        )
    return total


def shards(volume_init, measured, psf, offsets, counts):
    depth_here = volume_init.shape[0]
    tile_rows = volume_init.shape[1]
    tile_cols = volume_init.shape[2]
    pixels = volume_init.shape[3]
    slot_total = psf.shape[1]
    base_depth = lax.axis_index("depth") * depth_here
    local_offsets = lax.dynamic_slice_in_dim(offsets, base_depth, depth_here, 0)
    local_counts = lax.dynamic_slice_in_dim(counts, base_depth, depth_here, 0)
    slot_ids = jnp.arange(slot_total, dtype=jnp.int32)
    live = slot_ids[None, :] < local_counts[:, None]
    weights = jnp.where(live[:, :, None, None], psf, jnp.zeros_like(psf))
    shift_rows, shift_cols = split_offsets(local_offsets)
    all_rows = tile_rows * lax.axis_size("lat")
    row_ids = lax.axis_index("lat") * tile_rows + jnp.arange(tile_rows, dtype=jnp.int32)
    col_ids = jnp.arange(tile_cols, dtype=jnp.int32)
    coverages = []
    for plane_id in range(depth_here):
        source_rows = row_ids[None, :] - shift_rows[plane_id][:, None]
        source_cols = col_ids[None, :] - shift_cols[plane_id][:, None]
        inside_rows = (source_rows >= 0) & (source_rows < all_rows)
        inside_cols = (source_cols >= 0) & (source_cols < tile_cols)
        inside = (inside_rows[:, :, None] & inside_cols[:, None, :]).astype(jnp.float32)
        column_sums = jnp.sum(weights[plane_id].astype(jnp.float32), axis=2)
        coverages.append(
            jnp.einsum("kyx,kj->yxj", inside, column_sums, precision=lax.Precision.HIGHEST)
        )
    volume = volume_init
    for repeat in range(ITERS):
        extended = with_halo(volume.astype(jnp.bfloat16), (("lat", 1),), RY)
        padded = jnp.pad(extended, ((0, 0), (0, 0), (RX, RX), (0, 0)))
        partial_sensor = jnp.zeros((tile_rows, tile_cols, pixels), jnp.float32)
        for plane_id in range(depth_here):
            partial_sensor = partial_sensor + project(
                padded[plane_id],
                weights[plane_id],
                shift_rows[plane_id],
                shift_cols[plane_id],
                False,
            )
        sensor = lax.psum(partial_sensor, "depth")
        ratio = (measured / sensor).astype(jnp.bfloat16)
        ratio_ext = with_halo(ratio, (("lat", 0),), RY)
        ratio_pad = jnp.pad(ratio_ext, ((0, 0), (RX, RX), (0, 0)))
        updated = []
        for plane_id in range(depth_here):
            back = project(
                ratio_pad, weights[plane_id], -shift_rows[plane_id], -shift_cols[plane_id], True
            )
            updated.append(volume[plane_id] * back / coverages[plane_id])
        volume = jnp.stack(updated)
    return volume


def solution(mesh):
    return jax.shard_map(
        shards,
        mesh=mesh,
        in_specs=(
            P("depth", "lat", None, None),
            P("lat", None, None),
            P("depth", None, None, None),
            P(),
            P(),
        ),
        out_specs=P("depth", "lat", None, None),
        check_vma=False,
    )
```

profile of v0, /device:TPU:3, one launch (start us, length us, event | category | flops | bytes accessed | tf_op | source)
XLA Modules:
  0.0 168.0 jit_solution(4459511551675382461)
XLA Ops:
  6.5 1.0 convert_element_type.60
  7.5 3.7 %collective-permute-start = (bf16[4,2,16,128]{3,2,1,0:T(8,128)(2,1)S(1)}, bf16[4,2,16,128]{3,2,1,0:T(8,128)(2,1)}, u32[]{:S(2)}, u32[]{:S(2)}) collective-permute-start(bf16[4,2,16,128]{3,2,1,0:T(8,128)(2,1)S(1)} %get-tuple-element.19), channel_id=1, source_target_pairs={{0,1},{1,2},{2,3},{3,4},{4,5},{5,6},{6,7},{8,9},{9,10},{10,11},{11... | collective-permute-start | bytes 98312 | tf_op jit(solution)/shard_map/ppermute | solution.py:19
  11.2 1.9 %collective-permute-start.1 = (bf16[4,2,16,128]{3,2,1,0:T(8,128)(2,1)S(1)}, bf16[4,2,16,128]{3,2,1,0:T(8,128)(2,1)}, u32[]{:S(2)}, u32[]{:S(2)}) collective-permute-start(bf16[4,2,16,128]{3,2,1,0:T(8,128)(2,1)S(1)} %get-tuple-element.20), channel_id=1, source_target_pairs={{1,0},{2,1},{3,2},{4,3},{5,4},{6,5},{7,6},{9,8},{10,9},{11,10},{12... | collective-permute-start | bytes 98312 | tf_op jit(solution)/shard_map/ppermute | solution.py:21
  13.1 0.7 fusion.340
  13.9 0.6 slice_bitcast_fusion.213
  14.5 0.7 dynamic_slice.6
  15.3 2.5 %copy_select_fusion = bf16[4,13,128,128]{3,1,2,0:T(8,128)(2,1)S(1)} fusion(bf16[4,13,128,128]{3,2,1,0:T(8,128)(2,1)} %param.7, pred[4,13]{1,0:T(4,128)(4,1)S(1)} %iota_compare_fusion.12), kind=kLoop, calls=%fused_computation | loop fusion | flops 851968 | bytes 3407924 | tf_op jit(solution)/shard_map/jit(_where)/select_n | solution.py:75
  17.8 1.2 convert_reduce_fusion.3
  19.6 1.5 fusion.2
  21.1 1.5 fusion.1
  22.6 1.5 fusion
  24.1 1.5 fusion.4
  25.6 0.6 fusion.313
  26.2 1.5 fusion.5
  27.8 0.7 fusion.316
  28.4 1.5 fusion.6
  29.9 0.7 fusion.319
  30.6 1.5 fusion.7
  32.1 0.7 fusion.335
  32.9 0.9 fusion.281
  33.7 0.8 fusion.279
  34.6 0.8 fusion.277
  35.4 1.2 copy.892
  36.6 2.1 %copy.866 = bf16[128,25,128]{0,2,1:T(8,128)(2,1)S(1)} copy(bf16[128,25,128]{2,1,0:T(8,128)(2,1)} %fusion.2) | data formatting | bytes 1638400 | tf_op jit(solution)/shard_map/convert_element_type | solution.py:49
  38.8 2.1 %copy.840 = bf16[128,25,128]{0,2,1:T(8,128)(2,1)S(1)} copy(bf16[128,25,128]{2,1,0:T(8,128)(2,1)} %fusion.1) | data formatting | bytes 1638400 | tf_op jit(solution)/shard_map/convert_element_type | solution.py:49
  40.9 2.1 %copy.815 = bf16[128,25,128]{0,2,1:T(8,128)(2,1)S(1)} copy(bf16[128,25,128]{2,1,0:T(8,128)(2,1)} %fusion) | data formatting | bytes 1638400 | tf_op jit(solution)/shard_map/convert_element_type | solution.py:49
  43.1 0.9 select_maximum_fusion.5
  44.0 0.7 fusion.26
  44.7 0.7 fusion.30
  45.4 0.7 fusion.34
  46.1 0.7 fusion.38
  46.8 1.2 fusion.221
  48.0 33.3 %all-reduce.7.cloned.1.call-done = f32[8,16,128]{2,1,0:T(8,128)} async-done(((f32[8,16,128]{2,1,0:T(8,128)}), f32[8,16,128]{2,1,0:T(8,128)}) %all-reduce.7.cloned.1.call-update) | async-done | bytes 65552 | tf_op jit(solution)/shard_map/psum | solution.py:104
  81.4 1.0 divide_convert_fusion.1
  82.3 5.6 %collective-permute-start.2 = (bf16[2,16,128]{2,1,0:T(8,128)(2,1)S(1)}, bf16[2,16,128]{2,1,0:T(8,128)(2,1)S(1)}, u32[]{:S(2)}, u32[]{:S(2)}) collective-permute-start(bf16[2,16,128]{2,1,0:T(8,128)(2,1)S(1)} %get-tuple-element.23), channel_id=1, source_target_pairs={{0,1},{1,2},{2,3},{3,4},{4,5},{5,6},{6,7},{8,9},{9,10},{10,11},{11... | collective-permute-start | bytes 24584 | tf_op jit(solution)/shard_map/ppermute | solution.py:19
  88.0 2.1 %collective-permute-start.3 = (bf16[2,16,128]{2,1,0:T(8,128)(2,1)S(1)}, bf16[2,16,128]{2,1,0:T(8,128)(2,1)S(1)}, u32[]{:S(2)}, u32[]{:S(2)}) collective-permute-start(bf16[2,16,128]{2,1,0:T(8,128)(2,1)S(1)} %get-tuple-element.24), channel_id=1, source_target_pairs={{1,0},{2,1},{3,2},{4,3},{5,4},{6,5},{7,6},{9,8},{10,9},{11,10},{12... | collective-permute-start | bytes 24584 | tf_op jit(solution)/shard_map/ppermute | solution.py:21
  90.1 1.1 fusion.275
  91.2 2.7 %collective-permute-done.3 = bf16[2,16,128]{2,1,0:T(8,128)(2,1)S(1)} collective-permute-done((bf16[2,16,128]{2,1,0:T(8,128)(2,1)S(1)}, bf16[2,16,128]{2,1,0:T(8,128)(2,1)S(1)}, u32[]{:S(2)}, u32[]{:S(2)}) %collective-permute-start.3) | collective-permute-done | bytes 8224 | tf_op jit(solution)/shard_map/ppermute | solution.py:21
  93.9 2.0 %fusion.22 = f32[12,20,25,128]{3,1,2,0:T(8,128)S(1)} fusion(bf16[128,25,128]{0,1,2:T(8,128)(2,1)} %fusion.4, bf16[2,16,128]{2,1,0:T(8,128)(2,1)S(1)} %collective-permute-done.3, bf16[8,16,128]{2,1,0:T(8,128)(2,1)S(1)} %divide_convert_fusion.1, bf16[2,16,128]{2,1,0:T(8,128)(2,1)S(1)} %collective-permute-done.2), kind=kOutput, calls=%fused_computation.37 | convolution fusion | flops 196976640 | bytes 3940352 | tf_op jit(solution)/shard_map/dot_general | solution.py:50
  95.9 0.8 convert_bitcast_fusion.3
  96.6 0.7 fusion.20
  97.4 0.8 convert_bitcast_fusion.2
  98.2 0.7 fusion.16
  99.0 0.8 convert_bitcast_fusion.1
  99.8 0.7 fusion.12
  100.5 0.8 convert_bitcast_fusion
  101.3 1.9 %collective-permute-start.4 = (bf16[4,2,16,128]{3,2,1,0:T(8,128)(2,1)S(1)}, bf16[4,2,16,128]{3,2,1,0:T(8,128)(2,1)S(1)}, u32[]{:S(2)}, u32[]{:S(2)}) collective-permute-start(bf16[4,2,16,128]{3,2,1,0:T(8,128)(2,1)S(1)} %get-tuple-element.17), channel_id=1, source_target_pairs={{0,1},{1,2},{2,3},{3,4},{4,5},{5,6},{6,7},{8,9},{9,10},{10,11},{11... | collective-permute-start | bytes 98312 | tf_op jit(solution)/shard_map/ppermute | solution.py:19
  103.3 2.4 %collective-permute-start.5 = (bf16[4,2,16,128]{3,2,1,0:T(8,128)(2,1)S(1)}, bf16[4,2,16,128]{3,2,1,0:T(8,128)(2,1)S(1)}, u32[]{:S(2)}, u32[]{:S(2)}) collective-permute-start(bf16[4,2,16,128]{3,2,1,0:T(8,128)(2,1)S(1)} %get-tuple-element.18), channel_id=1, source_target_pairs={{1,0},{2,1},{3,2},{4,3},{5,4},{6,5},{7,6},{9,8},{10,9},{11,10},{12... | collective-permute-start | bytes 98312 | tf_op jit(solution)/shard_map/ppermute | solution.py:21
  105.7 3.7 %collective-permute-done.5 = bf16[4,2,16,128]{3,2,1,0:T(8,128)(2,1)S(1)} collective-permute-done((bf16[4,2,16,128]{3,2,1,0:T(8,128)(2,1)S(1)}, bf16[4,2,16,128]{3,2,1,0:T(8,128)(2,1)S(1)}, u32[]{:S(2)}, u32[]{:S(2)}) %collective-permute-start.5) | collective-permute-done | bytes 32800 | tf_op jit(solution)/shard_map/ppermute | solution.py:21
  109.5 0.7 fusion.32
  110.2 0.7 fusion.36
  110.9 0.7 fusion.28
  111.6 0.7 fusion.24
  112.3 1.2 fusion.106
  113.6 30.4 %all-reduce.9.cloned.1.call-done = f32[8,16,128]{2,1,0:T(8,128)} async-done(((f32[8,16,128]{2,1,0:T(8,128)}), f32[8,16,128]{2,1,0:T(8,128)}) %all-reduce.9.cloned.1.call-update) | async-done | bytes 65552 | tf_op jit(solution)/shard_map/psum | solution.py:104
  144.0 0.9 divide_convert_fusion
  144.9 5.6 %collective-permute-start.6 = (bf16[2,16,128]{2,1,0:T(8,128)(2,1)S(1)}, bf16[2,16,128]{2,1,0:T(8,128)(2,1)S(1)}, u32[]{:S(2)}, u32[]{:S(2)}) collective-permute-start(bf16[2,16,128]{2,1,0:T(8,128)(2,1)S(1)} %get-tuple-element.21), channel_id=1, source_target_pairs={{0,1},{1,2},{2,3},{3,4},{4,5},{5,6},{6,7},{8,9},{9,10},{10,11},{11... | collective-permute-start | bytes 24584 | tf_op jit(solution)/shard_map/ppermute | solution.py:19
  150.5 1.9 %collective-permute-start.7 = (bf16[2,16,128]{2,1,0:T(8,128)(2,1)S(1)}, bf16[2,16,128]{2,1,0:T(8,128)(2,1)S(1)}, u32[]{:S(2)}, u32[]{:S(2)}) collective-permute-start(bf16[2,16,128]{2,1,0:T(8,128)(2,1)S(1)} %get-tuple-element.22), channel_id=1, source_target_pairs={{1,0},{2,1},{3,2},{4,3},{5,4},{6,5},{7,6},{9,8},{10,9},{11,10},{12... | collective-permute-start | bytes 24584 | tf_op jit(solution)/shard_map/ppermute | solution.py:21
  152.5 3.9 %collective-permute-done.7 = bf16[2,16,128]{2,1,0:T(8,128)(2,1)S(1)} collective-permute-done((bf16[2,16,128]{2,1,0:T(8,128)(2,1)S(1)}, bf16[2,16,128]{2,1,0:T(8,128)(2,1)S(1)}, u32[]{:S(2)}, u32[]{:S(2)}) %collective-permute-start.7) | collective-permute-done | bytes 8224 | tf_op jit(solution)/shard_map/ppermute | solution.py:21
  156.4 0.7 fusion.8
  157.4 0.7 fusion.18
  158.5 0.7 fusion.14
  159.5 0.7 fusion.10
  160.4 0.7 pad_maximum_fusion
  (65 shorter events, 1.8 us)
Async XLA Ops:
  6.5 74.8 %all-reduce.7.cloned.1.call-start = ((), (), s32[]{:S(2)}) async-start(), calls=%async_computation | async-start | bytes 131072 | tf_op jit(solution)/shard_map/psum | solution.py:104
  7.5 35.5 %collective-permute-start = (bf16[4,2,16,128]{3,2,1,0:T(8,128)(2,1)S(1)}, bf16[4,2,16,128]{3,2,1,0:T(8,128)(2,1)}, u32[]{:S(2)}, u32[]{:S(2)}) collective-permute-start(bf16[4,2,16,128]{3,2,1,0:T(8,128)(2,1)S(1)} %get-tuple-element.19), channel_id=1, source_target_pairs={{0,1},{1,2},{2,3},{3,4},{4,5},{5,6},{6,7},{8,9},{9,10},{10,11},{11... | collective-permute-start | bytes 98312 | tf_op jit(solution)/shard_map/ppermute | solution.py:19
  11.2 31.9 %collective-permute-start.1 = (bf16[4,2,16,128]{3,2,1,0:T(8,128)(2,1)S(1)}, bf16[4,2,16,128]{3,2,1,0:T(8,128)(2,1)}, u32[]{:S(2)}, u32[]{:S(2)}) collective-permute-start(bf16[4,2,16,128]{3,2,1,0:T(8,128)(2,1)S(1)} %get-tuple-element.20), channel_id=1, source_target_pairs={{1,0},{2,1},{3,2},{4,3},{5,4},{6,5},{7,6},{9,8},{10,9},{11,10},{12... | collective-permute-start | bytes 98312 | tf_op jit(solution)/shard_map/ppermute | solution.py:21
  48.0 47.9 %copy-start.7 = (f32[4,8,16,128]{3,2,1,0:T(8,128)S(1)}, f32[4,8,16,128]{3,2,1,0:T(8,128)}, u32[]{:S(2)}) copy-start(f32[4,8,16,128]{3,2,1,0:T(8,128)} %param.5) | copy-start | bytes 786436
  48.0 96.1 %all-reduce.9.cloned.1.call-start = ((), (), s32[]{:S(2)}) async-start(), calls=%async_computation.1 | async-start | bytes 131072 | tf_op jit(solution)/shard_map/psum | solution.py:104
  81.3 14.5 %copy-start.12 = (f32[8,16,128]{2,1,0:T(8,128)S(1)}, f32[8,16,128]{2,1,0:T(8,128)}, u32[]{:S(2)}) copy-start(f32[8,16,128]{2,1,0:T(8,128)} %fusion.281) | copy-start | bytes 196612
  81.4 15.3 %copy-start.5 = (bf16[128,25,128]{0,1,2:T(8,128)(2,1)S(1)}, bf16[128,25,128]{0,1,2:T(8,128)(2,1)}, u32[]{:S(2)}) copy-start(bf16[128,25,128]{0,1,2:T(8,128)(2,1)} %fusion.5) | copy-start | bytes 2457604
  82.3 8.8 %collective-permute-start.2 = (bf16[2,16,128]{2,1,0:T(8,128)(2,1)S(1)}, bf16[2,16,128]{2,1,0:T(8,128)(2,1)S(1)}, u32[]{:S(2)}, u32[]{:S(2)}) collective-permute-start(bf16[2,16,128]{2,1,0:T(8,128)(2,1)S(1)} %get-tuple-element.23), channel_id=1, source_target_pairs={{0,1},{1,2},{2,3},{3,4},{4,5},{5,6},{6,7},{8,9},{9,10},{10,11},{11... | collective-permute-start | bytes 24584 | tf_op jit(solution)/shard_map/ppermute | solution.py:19
  88.0 5.9 %collective-permute-start.3 = (bf16[2,16,128]{2,1,0:T(8,128)(2,1)S(1)}, bf16[2,16,128]{2,1,0:T(8,128)(2,1)S(1)}, u32[]{:S(2)}, u32[]{:S(2)}) collective-permute-start(bf16[2,16,128]{2,1,0:T(8,128)(2,1)S(1)} %get-tuple-element.24), channel_id=1, source_target_pairs={{1,0},{2,1},{3,2},{4,3},{5,4},{6,5},{7,6},{9,8},{10,9},{11,10},{12... | collective-permute-start | bytes 24584 | tf_op jit(solution)/shard_map/ppermute | solution.py:21
  91.2 9.3 %copy-start.14 = (f32[8,16,128]{2,1,0:T(8,128)}, f32[8,16,128]{2,1,0:T(8,128)S(1)}, u32[]{:S(2)}) copy-start(f32[8,16,128]{2,1,0:T(8,128)S(1)} %fusion.275) | copy-start | bytes 196612
  95.8 1.6 copy-start.10
  95.8 2.4 %copy-start.3 = (bf16[128,25,128]{0,1,2:T(8,128)(2,1)S(1)}, bf16[128,25,128]{0,1,2:T(8,128)(2,1)}, u32[]{:S(2)}) copy-start(bf16[128,25,128]{0,1,2:T(8,128)(2,1)} %fusion.6) | copy-start | bytes 2457604
  97.4 1.6 copy-start.8
  97.4 2.3 %copy-start.1 = (bf16[128,25,128]{0,1,2:T(8,128)(2,1)S(1)}, bf16[128,25,128]{0,1,2:T(8,128)(2,1)}, u32[]{:S(2)}) copy-start(bf16[128,25,128]{0,1,2:T(8,128)(2,1)} %fusion.7) | copy-start | bytes 2457604
  101.3 4.3 %collective-permute-start.4 = (bf16[4,2,16,128]{3,2,1,0:T(8,128)(2,1)S(1)}, bf16[4,2,16,128]{3,2,1,0:T(8,128)(2,1)S(1)}, u32[]{:S(2)}, u32[]{:S(2)}) collective-permute-start(bf16[4,2,16,128]{3,2,1,0:T(8,128)(2,1)S(1)} %get-tuple-element.17), channel_id=1, source_target_pairs={{0,1},{1,2},{2,3},{3,4},{4,5},{5,6},{6,7},{8,9},{9,10},{10,11},{11... | collective-permute-start | bytes 98312 | tf_op jit(solution)/shard_map/ppermute | solution.py:19
  103.3 6.1 %collective-permute-start.5 = (bf16[4,2,16,128]{3,2,1,0:T(8,128)(2,1)S(1)}, bf16[4,2,16,128]{3,2,1,0:T(8,128)(2,1)S(1)}, u32[]{:S(2)}, u32[]{:S(2)}) collective-permute-start(bf16[4,2,16,128]{3,2,1,0:T(8,128)(2,1)S(1)} %get-tuple-element.18), channel_id=1, source_target_pairs={{1,0},{2,1},{3,2},{4,3},{5,4},{6,5},{7,6},{9,8},{10,9},{11,10},{12... | collective-permute-start | bytes 98312 | tf_op jit(solution)/shard_map/ppermute | solution.py:21
  112.3 31.7 %copy-start.20 = (f32[8,16,128]{2,1,0:T(8,128)S(1)}, f32[8,16,128]{2,1,0:T(8,128)}, u32[]{:S(2)}) copy-start(f32[8,16,128]{2,1,0:T(8,128)} %param.6) | copy-start | bytes 196612
  112.3 44.1 %copy-start = (bf16[128,25,128]{0,1,2:T(8,128)(2,1)S(1)}, bf16[128,25,128]{0,1,2:T(8,128)(2,1)}, u32[]{:S(2)}) copy-start(bf16[128,25,128]{0,1,2:T(8,128)(2,1)} %fusion.4) | copy-start | bytes 2457604
  113.6 43.6 %copy-start.13 = (f32[8,16,128]{2,1,0:T(8,128)S(1)}, f32[8,16,128]{2,1,0:T(8,128)}, u32[]{:S(2)}) copy-start(f32[8,16,128]{2,1,0:T(8,128)} %fusion.281) | copy-start | bytes 196612
  113.6 43.6 %copy-start.19 = (f32[8,16,128]{2,1,0:T(8,128)S(1)}, f32[8,16,128]{2,1,0:T(8,128)}, u32[]{:S(2)}) copy-start(f32[8,16,128]{2,1,0:T(8,128)} %get-tuple-element.10) | copy-start | bytes 196612
  113.6 43.8 %copy-start.6 = (bf16[128,25,128]{0,1,2:T(8,128)(2,1)S(1)}, bf16[128,25,128]{0,1,2:T(8,128)(2,1)}, u32[]{:S(2)}) copy-start(bf16[128,25,128]{0,1,2:T(8,128)(2,1)} %fusion.5) | copy-start | bytes 2457604
  144.9 7.6 %collective-permute-start.6 = (bf16[2,16,128]{2,1,0:T(8,128)(2,1)S(1)}, bf16[2,16,128]{2,1,0:T(8,128)(2,1)S(1)}, u32[]{:S(2)}, u32[]{:S(2)}) collective-permute-start(bf16[2,16,128]{2,1,0:T(8,128)(2,1)S(1)} %get-tuple-element.21), channel_id=1, source_target_pairs={{0,1},{1,2},{2,3},{3,4},{4,5},{5,6},{6,7},{8,9},{9,10},{10,11},{11... | collective-permute-start | bytes 24584 | tf_op jit(solution)/shard_map/ppermute | solution.py:19
  150.5 5.9 %collective-permute-start.7 = (bf16[2,16,128]{2,1,0:T(8,128)(2,1)S(1)}, bf16[2,16,128]{2,1,0:T(8,128)(2,1)S(1)}, u32[]{:S(2)}, u32[]{:S(2)}) collective-permute-start(bf16[2,16,128]{2,1,0:T(8,128)(2,1)S(1)} %get-tuple-element.22), channel_id=1, source_target_pairs={{1,0},{2,1},{3,2},{4,3},{5,4},{6,5},{7,6},{9,8},{10,9},{11,10},{12... | collective-permute-start | bytes 24584 | tf_op jit(solution)/shard_map/ppermute | solution.py:21
  157.2 1.0 copy-start.11
  157.2 1.0 copy-start.18
  157.2 1.3 copy-start.4
  158.1 1.1 copy-start.9
  158.1 1.1 copy-start.17
  158.2 1.3 copy-start.2
  159.2 1.0 copy-start.15
  159.2 1.0 copy-start.16
Sparse Core Ops, SparseCore 0:
  48.1 33.1 all-reduce.6
  113.7 30.2 all-reduce.8
where the time goes:
time: 169 us; the launch traced here: 168 us
  waiting for transfers between devices  74.1 us (44%)
  matrix products  27.4 us (16%)
  starting transfers between devices  25.2 us (15%)
  other arithmetic  18 us (11%)
  between operations  14 us (8%)
  local copies, waits for them, and re-layouts  9.22 us (5%)
    psum x2, waiting for transfers between devices, shards(): sensor = lax.psum(partial_sensor, 'depth')  63.7 us
    ppermute x4, starting transfers between devices, with_halo(): lax.ppermute(tail, axis, [(i, (i + 1) % count) for i in range(ends)])  16.9 us
    dot_general x16, matrix products, project(): jnp.dot(flat_plane, dense, preferred_element_type=jnp.float32)  12.6 us
    ppermute x4, waiting for transfers between devices, with_halo(): lax.ppermute(head, axis, [((i + 1) % count, i) for i in range(ends)])  10.3 us
    ppermute x4, starting transfers between devices, with_halo(): lax.ppermute(head, axis, [((i + 1) % count, i) for i in range(ends)])  8.33 us
    convert_element_type x4, local copies, waits for them, and re-layouts, project(): dense = dense.astype(jnp.bfloat16).reshape(pixels, span_all * pixels)  7.6 us
    dot_general x4, matrix products, project(): jnp.einsum('ko,kji->ioj', one_hot, block_values, precision=lax.Precision....  6.06 us
    dot_general x4, matrix products, project(): jnp.einsum('ko,kji->joi', one_hot, block_values, precision=lax.Precision....  5.1 us
  transfers between devices with their start and end apart: 10, of which 5 were waited for; matrix products, arithmetic and copies ran while one was open for 18% of the time, Pallas kernels for 0%

commit v1 on v0

--- a/solution.py
+++ b/solution.py
@@ -101,7 +101,7 @@
                 shift_cols[plane_id],
                 False,
             )
-        sensor = lax.psum(partial_sensor, "depth")
+        sensor = jnp.sum(lax.all_gather(partial_sensor, "depth"), axis=0)
         ratio = (measured / sensor).astype(jnp.bfloat16)
         ratio_ext = with_halo(ratio, (("lat", 0),), RY)
         ratio_pad = jnp.pad(ratio_ext, ((0, 0), (RX, RX), (0, 0)))

time: 169 us -> 116 us (0.69)
  waiting for transfers between devices: 74.1 us -> 10.3 us
  blocking collectives: 0 us -> 25.6 us
  between operations: 14 us -> 0.61 us
    psum x2 -> x0, waiting for transfers between devices: 63.7 us -> none  [shards(): sensor = lax.psum(partial_sensor, 'depth')]
    all_gather x0 -> x2, blocking collectives: none -> 25.6 us  [shards(): sensor = jnp.sum(lax.all_gather(partial_sensor, 'depth'), axis=0)]
  transfers between devices with their start and end apart: 10 -> 8, of which waited for: 5 -> 3; matrix products, arithmetic and copies ran while one was open for 18% -> 27% of each run, Pallas kernels for 0% -> 0%
where the time goes in v1:
time: 116 us; the launch traced here: 115 us
  matrix products  27.4 us (24%)
  blocking collectives  25.6 us (22%)
  starting transfers between devices  23.9 us (21%)
  other arithmetic  17.5 us (15%)
  waiting for transfers between devices  10.3 us (9%)
  local copies, waits for them, and re-layouts  9.22 us (8%)
    all_gather x2, blocking collectives, shards(): sensor = jnp.sum(lax.all_gather(partial_sensor, 'depth'), axis=0)  25.6 us
    ppermute x4, starting transfers between devices, with_halo(): lax.ppermute(tail, axis, [(i, (i + 1) % count) for i in range(ends)])  15.6 us
    dot_general x16, matrix products, project(): jnp.dot(flat_plane, dense, preferred_element_type=jnp.float32)  12.7 us
    ppermute x4, waiting for transfers between devices, with_halo(): lax.ppermute(head, axis, [((i + 1) % count, i) for i in range(ends)])  10.3 us
    ppermute x4, starting transfers between devices, with_halo(): lax.ppermute(head, axis, [((i + 1) % count, i) for i in range(ends)])  8.33 us
    convert_element_type x4, local copies, waits for them, and re-layouts, project(): dense = dense.astype(jnp.bfloat16).reshape(pixels, span_all * pixels)  7.6 us
    dot_general x4, matrix products, project(): jnp.einsum('ko,kji->ioj', one_hot, block_values, precision=lax.Precision....  6.09 us
    dot_general x4, matrix products, project(): jnp.einsum('ko,kji->joi', one_hot, block_values, precision=lax.Precision....  5.12 us
  transfers between devices with their start and end apart: 8, of which 3 were waited for; matrix products, arithmetic and copies ran while one was open for 27% of the time, Pallas kernels for 0%

profile of v1, /device:TPU:3, one launch (start us, length us, event | category | flops | bytes accessed | tf_op | source)
XLA Modules:
  0.0 114.6 jit_solution(3182926670509095059)
XLA Ops:
  0.0 1.0 convert_element_type.60
  1.0 3.7 %collective-permute-start = (bf16[4,2,16,128]{3,2,1,0:T(8,128)(2,1)S(1)}, bf16[4,2,16,128]{3,2,1,0:T(8,128)(2,1)}, u32[]{:S(2)}, u32[]{:S(2)}) collective-permute-start(bf16[4,2,16,128]{3,2,1,0:T(8,128)(2,1)S(1)} %get-tuple-element.19), channel_id=1, source_target_pairs={{0,1},{1,2},{2,3},{3,4},{4,5},{5,6},{6,7},{8,9},{9,10},{10,11},{11... | collective-permute-start | bytes 98312 | tf_op jit(solution)/shard_map/ppermute | solution.py:19
  4.7 1.9 %collective-permute-start.1 = (bf16[4,2,16,128]{3,2,1,0:T(8,128)(2,1)S(1)}, bf16[4,2,16,128]{3,2,1,0:T(8,128)(2,1)}, u32[]{:S(2)}, u32[]{:S(2)}) collective-permute-start(bf16[4,2,16,128]{3,2,1,0:T(8,128)(2,1)S(1)} %get-tuple-element.20), channel_id=1, source_target_pairs={{1,0},{2,1},{3,2},{4,3},{5,4},{6,5},{7,6},{9,8},{10,9},{11,10},{12... | collective-permute-start | bytes 98312 | tf_op jit(solution)/shard_map/ppermute | solution.py:21
  6.6 0.7 fusion.340
  7.3 0.6 slice_bitcast_fusion.213
  8.0 0.7 dynamic_slice.6
  8.8 2.5 %copy_select_fusion = bf16[4,13,128,128]{3,1,2,0:T(8,128)(2,1)S(1)} fusion(bf16[4,13,128,128]{3,2,1,0:T(8,128)(2,1)} %param.7, pred[4,13]{1,0:T(4,128)(4,1)S(1)} %iota_compare_fusion.12), kind=kLoop, calls=%fused_computation | loop fusion | flops 851968 | bytes 3407924 | tf_op jit(solution)/shard_map/jit(_where)/select_n | solution.py:75
  11.2 1.2 %convert_reduce_fusion.3 = (f32[13,128]{0,1:T(8,128)S(1)}, f32[13,128]{0,1:T(8,128)}, f32[13,128]{0,1:T(8,128)S(1)}, f32[13,128]{0,1:T(8,128)S(1)}) fusion(bf16[4,13,128,128]{3,1,2,0:T(8,128)(2,1)S(1)} %copy_select_fusion), kind=kLoop, calls=%fused_computation.20 | loop fusion | flops 1697280 | bytes 1730560 | tf_op jit(solution)/shard_map/reduce_sum | solution.py:87
  13.0 1.6 %fusion.2 = bf16[128,25,128]{2,1,0:T(8,128)(2,1)} fusion(bf16[4,13,128,128]{3,1,2,0:T(8,128)(2,1)S(1)} %copy_select_fusion, s32[13]{0:T(128)S(1)} %get-tuple-element.30), kind=kOutput, calls=%fused_computation.11 | convolution fusion | flops 11059525 | bytes 1344000 | tf_op jit(solution)/shard_map/ko,kji->joi/dot_general | solution.py:48
  14.6 1.5 %fusion.1 = bf16[128,25,128]{2,1,0:T(8,128)(2,1)} fusion(bf16[4,13,128,128]{3,1,2,0:T(8,128)(2,1)S(1)} %copy_select_fusion, s32[13]{0:T(128)S(1)} %get-tuple-element.32), kind=kOutput, calls=%fused_computation.10 | convolution fusion | flops 11059525 | bytes 1344000 | tf_op jit(solution)/shard_map/ko,kji->joi/dot_general | solution.py:48
  16.1 1.5 %fusion = bf16[128,25,128]{2,1,0:T(8,128)(2,1)} fusion(bf16[4,13,128,128]{3,1,2,0:T(8,128)(2,1)S(1)} %copy_select_fusion, s32[13]{0:T(128)S(1)} %get-tuple-element.34), kind=kOutput, calls=%fused_computation.9 | convolution fusion | flops 11059525 | bytes 1344000 | tf_op jit(solution)/shard_map/ko,kji->joi/dot_general | solution.py:48
  17.6 1.5 %fusion.4 = bf16[128,25,128]{0,1,2:T(8,128)(2,1)} fusion(bf16[4,13,128,128]{3,1,2,0:T(8,128)(2,1)S(1)} %copy_select_fusion, s32[13]{0:T(128)S(1)} %get-tuple-element.27), kind=kOutput, calls=%fused_computation.13 | convolution fusion | flops 11059525 | bytes 1344000 | tf_op jit(solution)/shard_map/ko,kji->ioj/dot_general | solution.py:46
  19.1 0.6 fusion.313
  19.8 1.5 %fusion.5 = bf16[128,25,128]{0,1,2:T(8,128)(2,1)} fusion(bf16[4,13,128,128]{3,1,2,0:T(8,128)(2,1)S(1)} %copy_select_fusion, s32[13]{0:T(128)S(1)} %get-tuple-element.33), kind=kOutput, calls=%fused_computation.14 | convolution fusion | flops 11059525 | bytes 1344000 | tf_op jit(solution)/shard_map/ko,kji->ioj/dot_general | solution.py:46
  21.3 0.6 fusion.316
  21.9 1.5 %fusion.6 = bf16[128,25,128]{0,1,2:T(8,128)(2,1)} fusion(bf16[4,13,128,128]{3,1,2,0:T(8,128)(2,1)S(1)} %copy_select_fusion, s32[13]{0:T(128)S(1)} %get-tuple-element.31), kind=kOutput, calls=%fused_computation.15 | convolution fusion | flops 11059525 | bytes 1344000 | tf_op jit(solution)/shard_map/ko,kji->ioj/dot_general | solution.py:46
  23.5 0.6 fusion.319
  24.1 1.5 %fusion.7 = bf16[128,25,128]{0,1,2:T(8,128)(2,1)} fusion(bf16[4,13,128,128]{3,1,2,0:T(8,128)(2,1)S(1)} %copy_select_fusion, s32[13]{0:T(128)S(1)} %get-tuple-element.29), kind=kOutput, calls=%fused_computation.16 | convolution fusion | flops 11059525 | bytes 1344000 | tf_op jit(solution)/shard_map/ko,kji->ioj/dot_general | solution.py:46
  25.6 0.8 fusion.335
  26.4 0.8 fusion.281
  27.2 0.8 fusion.279
  28.0 0.8 fusion.277
  28.9 1.2 %copy.892 = bf16[128,25,128]{0,2,1:T(8,128)(2,1)S(1)} copy(bf16[128,25,128]{2,1,0:T(8,128)(2,1)S(1)} %fusion.3) | data formatting | bytes 1638400 | tf_op jit(solution)/shard_map/convert_element_type | solution.py:49
  30.0 2.1 %copy.866 = bf16[128,25,128]{0,2,1:T(8,128)(2,1)S(1)} copy(bf16[128,25,128]{2,1,0:T(8,128)(2,1)} %fusion.2) | data formatting | bytes 1638400 | tf_op jit(solution)/shard_map/convert_element_type | solution.py:49
  32.2 2.1 %copy.840 = bf16[128,25,128]{0,2,1:T(8,128)(2,1)S(1)} copy(bf16[128,25,128]{2,1,0:T(8,128)(2,1)} %fusion.1) | data formatting | bytes 1638400 | tf_op jit(solution)/shard_map/convert_element_type | solution.py:49
  34.4 2.1 %copy.815 = bf16[128,25,128]{0,2,1:T(8,128)(2,1)S(1)} copy(bf16[128,25,128]{2,1,0:T(8,128)(2,1)} %fusion) | data formatting | bytes 1638400 | tf_op jit(solution)/shard_map/convert_element_type | solution.py:49
  36.5 0.9 select_maximum_fusion.5
  37.4 0.7 fusion.26
  38.1 0.7 fusion.30
  38.8 0.7 fusion.34
  39.5 0.7 fusion.38
  40.2 0.6 fusion.221
  40.8 13.2 %all_gather.8 = f32[4,8,16,128]{3,2,1,0:T(8,128)} all-gather(f32[1,8,16,128]{3,2,1,0:T(8,128)S(1)} %fusion.221), channel_id=1, replica_groups=mesh['depth'=4,'lat'=8] {'depth'}, dimensions={0}, use_global_device_ids=true | all-gather | bytes 327680 | tf_op jit(solution)/shard_map/all_gather | solution.py:104
  54.0 1.6 %reduce_sum.54 = f32[8,16,128]{2,1,0:T(8,128)} reduce(f32[4,8,16,128]{3,2,1,0:T(8,128)} %all_gather.8, f32[]{:T(128)} %constant.48.clone.1), dimensions={0}, to_apply=%region_0.1 | reduce | flops 49152 | bytes 327684 | tf_op jit(solution)/shard_map/reduce_sum | solution.py:104
  55.6 1.0 divide_convert_fusion.1
  56.6 6.3 %collective-permute-start.2 = (bf16[2,16,128]{2,1,0:T(8,128)(2,1)S(1)}, bf16[2,16,128]{2,1,0:T(8,128)(2,1)S(1)}, u32[]{:S(2)}, u32[]{:S(2)}) collective-permute-start(bf16[2,16,128]{2,1,0:T(8,128)(2,1)S(1)} %get-tuple-element.23), channel_id=1, source_target_pairs={{0,1},{1,2},{2,3},{3,4},{4,5},{5,6},{6,7},{8,9},{9,10},{10,11},{11... | collective-permute-start | bytes 24584 | tf_op jit(solution)/shard_map/ppermute | solution.py:19
  62.9 2.1 %collective-permute-start.3 = (bf16[2,16,128]{2,1,0:T(8,128)(2,1)S(1)}, bf16[2,16,128]{2,1,0:T(8,128)(2,1)S(1)}, u32[]{:S(2)}, u32[]{:S(2)}) collective-permute-start(bf16[2,16,128]{2,1,0:T(8,128)(2,1)S(1)} %get-tuple-element.24), channel_id=1, source_target_pairs={{1,0},{2,1},{3,2},{4,3},{5,4},{6,5},{7,6},{9,8},{10,9},{11,10},{12... | collective-permute-start | bytes 24584 | tf_op jit(solution)/shard_map/ppermute | solution.py:21
  65.1 1.1 fusion.275
  66.1 2.7 %collective-permute-done.3 = bf16[2,16,128]{2,1,0:T(8,128)(2,1)S(1)} collective-permute-done((bf16[2,16,128]{2,1,0:T(8,128)(2,1)S(1)}, bf16[2,16,128]{2,1,0:T(8,128)(2,1)S(1)}, u32[]{:S(2)}, u32[]{:S(2)}) %collective-permute-start.3) | collective-permute-done | bytes 8224 | tf_op jit(solution)/shard_map/ppermute | solution.py:21
  68.8 2.0 %fusion.22 = f32[12,20,25,128]{3,1,2,0:T(8,128)S(1)} fusion(bf16[128,25,128]{0,1,2:T(8,128)(2,1)} %fusion.4, bf16[2,16,128]{2,1,0:T(8,128)(2,1)S(1)} %collective-permute-done.3, bf16[8,16,128]{2,1,0:T(8,128)(2,1)S(1)} %divide_convert_fusion.1, bf16[2,16,128]{2,1,0:T(8,128)(2,1)S(1)} %collective-permute-done.2), kind=kOutput, calls=%fused_computation.37 | convolution fusion | flops 196976640 | bytes 3940352 | tf_op jit(solution)/shard_map/dot_general | solution.py:50
  70.8 0.8 convert_bitcast_fusion.3
  71.6 0.7 fusion.20
  72.4 0.8 convert_bitcast_fusion.2
  73.2 0.7 fusion.16
  74.0 0.8 convert_bitcast_fusion.1
  74.8 0.7 fusion.12
  75.5 0.8 convert_bitcast_fusion
  76.3 1.9 %collective-permute-start.4 = (bf16[4,2,16,128]{3,2,1,0:T(8,128)(2,1)S(1)}, bf16[4,2,16,128]{3,2,1,0:T(8,128)(2,1)S(1)}, u32[]{:S(2)}, u32[]{:S(2)}) collective-permute-start(bf16[4,2,16,128]{3,2,1,0:T(8,128)(2,1)S(1)} %get-tuple-element.17), channel_id=1, source_target_pairs={{0,1},{1,2},{2,3},{3,4},{4,5},{5,6},{6,7},{8,9},{9,10},{10,11},{11... | collective-permute-start | bytes 98312 | tf_op jit(solution)/shard_map/ppermute | solution.py:19
  78.3 2.4 %collective-permute-start.5 = (bf16[4,2,16,128]{3,2,1,0:T(8,128)(2,1)S(1)}, bf16[4,2,16,128]{3,2,1,0:T(8,128)(2,1)S(1)}, u32[]{:S(2)}, u32[]{:S(2)}) collective-permute-start(bf16[4,2,16,128]{3,2,1,0:T(8,128)(2,1)S(1)} %get-tuple-element.18), channel_id=1, source_target_pairs={{1,0},{2,1},{3,2},{4,3},{5,4},{6,5},{7,6},{9,8},{10,9},{11,10},{12... | collective-permute-start | bytes 98312 | tf_op jit(solution)/shard_map/ppermute | solution.py:21
  80.7 3.7 %collective-permute-done.5 = bf16[4,2,16,128]{3,2,1,0:T(8,128)(2,1)S(1)} collective-permute-done((bf16[4,2,16,128]{3,2,1,0:T(8,128)(2,1)S(1)}, bf16[4,2,16,128]{3,2,1,0:T(8,128)(2,1)S(1)}, u32[]{:S(2)}, u32[]{:S(2)}) %collective-permute-start.5) | collective-permute-done | bytes 32800 | tf_op jit(solution)/shard_map/ppermute | solution.py:21
  84.5 0.7 fusion.32
  85.2 0.7 fusion.36
  85.9 0.7 fusion.28
  86.6 0.7 fusion.24
  87.4 0.6 fusion.106
  88.0 12.3 %all_gather.9 = f32[4,8,16,128]{3,2,1,0:T(8,128)S(1)} all-gather(f32[1,8,16,128]{3,2,1,0:T(8,128)S(1)} %fusion.106), channel_id=1, replica_groups=mesh['depth'=4,'lat'=8] {'depth'}, dimensions={0}, use_global_device_ids=true | all-gather | bytes 327680 | tf_op jit(solution)/shard_map/all_gather | solution.py:104
  100.4 3.6 %collective-permute-start.6 = (bf16[2,16,128]{2,1,0:T(8,128)(2,1)S(1)}, bf16[2,16,128]{2,1,0:T(8,128)(2,1)S(1)}, u32[]{:S(2)}, u32[]{:S(2)}) collective-permute-start(bf16[2,16,128]{2,1,0:T(8,128)(2,1)S(1)} %get-tuple-element.21), channel_id=1, source_target_pairs={{0,1},{1,2},{2,3},{3,4},{4,5},{5,6},{6,7},{8,9},{9,10},{10,11},{11... | collective-permute-start | bytes 24584 | tf_op jit(solution)/shard_map/ppermute | solution.py:19
  104.0 1.9 %collective-permute-start.7 = (bf16[2,16,128]{2,1,0:T(8,128)(2,1)S(1)}, bf16[2,16,128]{2,1,0:T(8,128)(2,1)S(1)}, u32[]{:S(2)}, u32[]{:S(2)}) collective-permute-start(bf16[2,16,128]{2,1,0:T(8,128)(2,1)S(1)} %get-tuple-element.22), channel_id=1, source_target_pairs={{1,0},{2,1},{3,2},{4,3},{5,4},{6,5},{7,6},{9,8},{10,9},{11,10},{12... | collective-permute-start | bytes 24584 | tf_op jit(solution)/shard_map/ppermute | solution.py:21
  106.0 3.9 %collective-permute-done.7 = bf16[2,16,128]{2,1,0:T(8,128)(2,1)S(1)} collective-permute-done((bf16[2,16,128]{2,1,0:T(8,128)(2,1)S(1)}, bf16[2,16,128]{2,1,0:T(8,128)(2,1)S(1)}, u32[]{:S(2)}, u32[]{:S(2)}) %collective-permute-start.7) | collective-permute-done | bytes 8224 | tf_op jit(solution)/shard_map/ppermute | solution.py:21
  109.9 0.7 fusion.8
  110.9 0.7 fusion.18
  111.9 0.7 fusion.14
  113.0 0.7 fusion.10
  113.9 0.7 pad_maximum_fusion
  (63 shorter events, 1.8 us)
Async XLA Ops:
  1.0 35.5 %collective-permute-start = (bf16[4,2,16,128]{3,2,1,0:T(8,128)(2,1)S(1)}, bf16[4,2,16,128]{3,2,1,0:T(8,128)(2,1)}, u32[]{:S(2)}, u32[]{:S(2)}) collective-permute-start(bf16[4,2,16,128]{3,2,1,0:T(8,128)(2,1)S(1)} %get-tuple-element.19), channel_id=1, source_target_pairs={{0,1},{1,2},{2,3},{3,4},{4,5},{5,6},{6,7},{8,9},{9,10},{10,11},{11... | collective-permute-start | bytes 98312 | tf_op jit(solution)/shard_map/ppermute | solution.py:19
  4.7 31.8 %collective-permute-start.1 = (bf16[4,2,16,128]{3,2,1,0:T(8,128)(2,1)S(1)}, bf16[4,2,16,128]{3,2,1,0:T(8,128)(2,1)}, u32[]{:S(2)}, u32[]{:S(2)}) collective-permute-start(bf16[4,2,16,128]{3,2,1,0:T(8,128)(2,1)S(1)} %get-tuple-element.20), channel_id=1, source_target_pairs={{1,0},{2,1},{3,2},{4,3},{5,4},{6,5},{7,6},{9,8},{10,9},{11,10},{12... | collective-permute-start | bytes 98312 | tf_op jit(solution)/shard_map/ppermute | solution.py:21
  40.8 30.0 %copy-start.7 = (f32[4,8,16,128]{3,2,1,0:T(8,128)S(1)}, f32[4,8,16,128]{3,2,1,0:T(8,128)}, u32[]{:S(2)}) copy-start(f32[4,8,16,128]{3,2,1,0:T(8,128)} %param.5) | copy-start | bytes 786436
  55.6 15.2 %copy-start.12 = (f32[8,16,128]{2,1,0:T(8,128)S(1)}, f32[8,16,128]{2,1,0:T(8,128)}, u32[]{:S(2)}) copy-start(f32[8,16,128]{2,1,0:T(8,128)} %fusion.281) | copy-start | bytes 196612
  55.6 16.0 %copy-start.5 = (bf16[128,25,128]{0,1,2:T(8,128)(2,1)S(1)}, bf16[128,25,128]{0,1,2:T(8,128)(2,1)}, u32[]{:S(2)}) copy-start(bf16[128,25,128]{0,1,2:T(8,128)(2,1)} %fusion.5) | copy-start | bytes 2457604
  56.6 9.5 %collective-permute-start.2 = (bf16[2,16,128]{2,1,0:T(8,128)(2,1)S(1)}, bf16[2,16,128]{2,1,0:T(8,128)(2,1)S(1)}, u32[]{:S(2)}, u32[]{:S(2)}) collective-permute-start(bf16[2,16,128]{2,1,0:T(8,128)(2,1)S(1)} %get-tuple-element.23), channel_id=1, source_target_pairs={{0,1},{1,2},{2,3},{3,4},{4,5},{5,6},{6,7},{8,9},{9,10},{10,11},{11... | collective-permute-start | bytes 24584 | tf_op jit(solution)/shard_map/ppermute | solution.py:19
  62.9 5.9 %collective-permute-start.3 = (bf16[2,16,128]{2,1,0:T(8,128)(2,1)S(1)}, bf16[2,16,128]{2,1,0:T(8,128)(2,1)S(1)}, u32[]{:S(2)}, u32[]{:S(2)}) collective-permute-start(bf16[2,16,128]{2,1,0:T(8,128)(2,1)S(1)} %get-tuple-element.24), channel_id=1, source_target_pairs={{1,0},{2,1},{3,2},{4,3},{5,4},{6,5},{7,6},{9,8},{10,9},{11,10},{12... | collective-permute-start | bytes 24584 | tf_op jit(solution)/shard_map/ppermute | solution.py:21
  66.1 9.4 %copy-start.14 = (f32[8,16,128]{2,1,0:T(8,128)}, f32[8,16,128]{2,1,0:T(8,128)S(1)}, u32[]{:S(2)}) copy-start(f32[8,16,128]{2,1,0:T(8,128)S(1)} %fusion.275) | copy-start | bytes 196612
  70.8 1.6 %copy-start.10 = (f32[8,16,128]{2,1,0:T(8,128)S(1)}, f32[8,16,128]{2,1,0:T(8,128)}, u32[]{:S(2)}) copy-start(f32[8,16,128]{2,1,0:T(8,128)} %fusion.279) | copy-start | bytes 196612
  70.8 2.4 %copy-start.3 = (bf16[128,25,128]{0,1,2:T(8,128)(2,1)S(1)}, bf16[128,25,128]{0,1,2:T(8,128)(2,1)}, u32[]{:S(2)}) copy-start(bf16[128,25,128]{0,1,2:T(8,128)(2,1)} %fusion.6) | copy-start | bytes 2457604
  72.4 1.6 %copy-start.8 = (f32[8,16,128]{2,1,0:T(8,128)S(1)}, f32[8,16,128]{2,1,0:T(8,128)}, u32[]{:S(2)}) copy-start(f32[8,16,128]{2,1,0:T(8,128)} %fusion.277) | copy-start | bytes 196612
  72.4 2.4 %copy-start.1 = (bf16[128,25,128]{0,1,2:T(8,128)(2,1)S(1)}, bf16[128,25,128]{0,1,2:T(8,128)(2,1)}, u32[]{:S(2)}) copy-start(bf16[128,25,128]{0,1,2:T(8,128)(2,1)} %fusion.7) | copy-start | bytes 2457604
  76.3 4.3 %collective-permute-start.4 = (bf16[4,2,16,128]{3,2,1,0:T(8,128)(2,1)S(1)}, bf16[4,2,16,128]{3,2,1,0:T(8,128)(2,1)S(1)}, u32[]{:S(2)}, u32[]{:S(2)}) collective-permute-start(bf16[4,2,16,128]{3,2,1,0:T(8,128)(2,1)S(1)} %get-tuple-element.17), channel_id=1, source_target_pairs={{0,1},{1,2},{2,3},{3,4},{4,5},{5,6},{6,7},{8,9},{9,10},{10,11},{11... | collective-permute-start | bytes 98312 | tf_op jit(solution)/shard_map/ppermute | solution.py:19
  78.3 6.1 %collective-permute-start.5 = (bf16[4,2,16,128]{3,2,1,0:T(8,128)(2,1)S(1)}, bf16[4,2,16,128]{3,2,1,0:T(8,128)(2,1)S(1)}, u32[]{:S(2)}, u32[]{:S(2)}) collective-permute-start(bf16[4,2,16,128]{3,2,1,0:T(8,128)(2,1)S(1)} %get-tuple-element.18), channel_id=1, source_target_pairs={{1,0},{2,1},{3,2},{4,3},{5,4},{6,5},{7,6},{9,8},{10,9},{11,10},{12... | collective-permute-start | bytes 98312 | tf_op jit(solution)/shard_map/ppermute | solution.py:21
  87.3 13.0 %copy-start.20 = (f32[8,16,128]{2,1,0:T(8,128)S(1)}, f32[8,16,128]{2,1,0:T(8,128)}, u32[]{:S(2)}) copy-start(f32[8,16,128]{2,1,0:T(8,128)} %param.6) | copy-start | bytes 196612
  87.3 22.6 %copy-start = (bf16[128,25,128]{0,1,2:T(8,128)(2,1)S(1)}, bf16[128,25,128]{0,1,2:T(8,128)(2,1)}, u32[]{:S(2)}) copy-start(bf16[128,25,128]{0,1,2:T(8,128)(2,1)} %fusion.4) | copy-start | bytes 2457604
  87.9 22.7 %copy-start.13 = (f32[8,16,128]{2,1,0:T(8,128)S(1)}, f32[8,16,128]{2,1,0:T(8,128)}, u32[]{:S(2)}) copy-start(f32[8,16,128]{2,1,0:T(8,128)} %fusion.281) | copy-start | bytes 196612
  87.9 22.7 %copy-start.19 = (f32[8,16,128]{2,1,0:T(8,128)S(1)}, f32[8,16,128]{2,1,0:T(8,128)}, u32[]{:S(2)}) copy-start(f32[8,16,128]{2,1,0:T(8,128)} %get-tuple-element.10) | copy-start | bytes 196612
  88.0 22.9 %copy-start.6 = (bf16[128,25,128]{0,1,2:T(8,128)(2,1)S(1)}, bf16[128,25,128]{0,1,2:T(8,128)(2,1)}, u32[]{:S(2)}) copy-start(bf16[128,25,128]{0,1,2:T(8,128)(2,1)} %fusion.5) | copy-start | bytes 2457604
  100.4 5.6 %collective-permute-start.6 = (bf16[2,16,128]{2,1,0:T(8,128)(2,1)S(1)}, bf16[2,16,128]{2,1,0:T(8,128)(2,1)S(1)}, u32[]{:S(2)}, u32[]{:S(2)}) collective-permute-start(bf16[2,16,128]{2,1,0:T(8,128)(2,1)S(1)} %get-tuple-element.21), channel_id=1, source_target_pairs={{0,1},{1,2},{2,3},{3,4},{4,5},{5,6},{6,7},{8,9},{9,10},{10,11},{11... | collective-permute-start | bytes 24584 | tf_op jit(solution)/shard_map/ppermute | solution.py:19
  104.0 5.9 %collective-permute-start.7 = (bf16[2,16,128]{2,1,0:T(8,128)(2,1)S(1)}, bf16[2,16,128]{2,1,0:T(8,128)(2,1)S(1)}, u32[]{:S(2)}, u32[]{:S(2)}) collective-permute-start(bf16[2,16,128]{2,1,0:T(8,128)(2,1)S(1)} %get-tuple-element.22), channel_id=1, source_target_pairs={{1,0},{2,1},{3,2},{4,3},{5,4},{6,5},{7,6},{9,8},{10,9},{11,10},{12... | collective-permute-start | bytes 24584 | tf_op jit(solution)/shard_map/ppermute | solution.py:21
  110.6 1.0 copy-start.11
  110.7 1.0 copy-start.18
  110.7 1.3 %copy-start.4 = (bf16[128,25,128]{0,1,2:T(8,128)(2,1)S(1)}, bf16[128,25,128]{0,1,2:T(8,128)(2,1)}, u32[]{:S(2)}) copy-start(bf16[128,25,128]{0,1,2:T(8,128)(2,1)} %fusion.6) | copy-start | bytes 2457604
  111.6 1.1 copy-start.9
  111.6 1.1 copy-start.17
  111.7 1.3 %copy-start.2 = (bf16[128,25,128]{0,1,2:T(8,128)(2,1)S(1)}, bf16[128,25,128]{0,1,2:T(8,128)(2,1)}, u32[]{:S(2)}) copy-start(bf16[128,25,128]{0,1,2:T(8,128)(2,1)} %fusion.7) | copy-start | bytes 2457604
  112.7 1.0 copy-start.15
  112.7 1.0 copy-start.16
